TPU v7x, 512 devices: a whole 4x4x16 slice. The times are simulated.
512 devices in a mesh: rep: 2 (over core), row: 16 (over y, x), col: 16 (over z).
Axes of the slice: x: 4, y: 4, z: 16, core: 2. Of those that a mesh axis runs over, the one named last changes fastest.
Arguments:
- residual: bfloat16 [16384, 2048], P(('rep', 'row'), 'col'), may hold values from -6 to 6
- post_gain: float32 [2048], replicated, may hold values from 0.25 to 1.75
- w_gate: bfloat16 [2048, 6144], P('row', 'col'), may hold values from -0.125 to 0.125
- w_up: bfloat16 [2048, 6144], P('row', 'col'), may hold values from -0.125 to 0.125
- w_down: bfloat16 [6144, 2048], P('col', 'row'), may hold values from -0.078125 to 0.078125
- next_gain: float32 [2048], replicated, may hold values from 0.25 to 1.75
- w_qkv: bfloat16 [2048, 4096], P('row', 'col'), may hold values from -0.125 to 0.125
- q_gain: float32 [128], replicated, may hold values from 0.25 to 1.75
- k_gain: float32 [128], replicated, may hold values from 0.25 to 1.75
- source: int32 [16384], P(('rep', 'row')), may hold values from 0 to 16383, as said below
Outputs:
- moved_residual: bfloat16 [16384, 2048], P(('rep', 'row'), 'col')
- moved_qkv: bfloat16 [16384, 4096], P(('rep', 'row'), 'col')
Inputs may be any that keep to these rules, and one draw needn't show every extreme that they name: source is a permutation of all rows. Rows are grouped in blocks of 512 (block b holds rows b * 512 to (b + 1) * 512 - 1, blocks of replica 0 first); output block b takes its rows from input block b or from the block of the same row index in the other replica, at most 128 of them from the other replica, and some block takes exactly 128. A block takes as many rows from the other replica as it gives to it.
All inputs are finite; a program needn't handle non-finite values.
Results may differ from a plain program's by a relative error of at most 0.0065.
Values may be sent and summed in bfloat16 or wider, within the bound.
A program may use at most 64 MiB of HBM per device.

v0:
```python
import jax
import jax.numpy as jnp
from jax import lax
from jax.sharding import PartitionSpec as P

HEADS = 16
KV_HEADS = 8
HD = 128


epsilon = 1e-06


def swapped(x, axis, apart):
    return lax.ppermute(x, axis, [(i, i ^ 1 << apart) for i in range(lax.axis_size(axis))])


def normalize(values, gain):
    scale = lax.rsqrt(jnp.mean(values * values, axis=-1, keepdims=True) + epsilon)
    return values * scale * gain


def per_device(residual, post_gain, w_gate, w_up, w_down, next_gain, w_qkv, q_gain, k_gain, source):
    tok_rows = residual.shape[0]
    col_index = lax.axis_index("col")
    gathered = lax.all_gather(residual, "col", axis=1, tiled=True)
    stream = gathered.astype(jnp.float32)
    normed = normalize(stream, post_gain).astype(jnp.bfloat16)
    columns = normed
    gate_proj = jnp.dot(
        columns,
        lax.all_gather(w_gate, "row", axis=0, tiled=True),
        preferred_element_type=jnp.float32,
    )
    up_proj = jnp.dot(
        columns, lax.all_gather(w_up, "row", axis=0, tiled=True), preferred_element_type=jnp.float32
    )
    hidden = (jax.nn.silu(gate_proj) * up_proj).astype(jnp.bfloat16)
    partial_value = jnp.dot(
        hidden,
        lax.all_gather(w_down, "row", axis=1, tiled=True),
        preferred_element_type=jnp.float32,
    )
    mlp_share = lax.psum_scatter(partial_value, "col", scatter_dimension=1, tiled=True)
    resid_own = (residual.astype(jnp.float32) + mlp_share).astype(jnp.bfloat16)
    resid_full = lax.all_gather(resid_own, "col", axis=1, tiled=True)
    next_normed = normalize(resid_full.astype(jnp.float32), next_gain).astype(jnp.bfloat16)
    proj_width = w_qkv.shape[1]
    columns = next_normed
    projected = jnp.dot(
        columns,
        lax.all_gather(w_qkv, "row", axis=0, tiled=True),
        preferred_element_type=jnp.float32,
    )
    head_count = proj_width // HD
    per_head = projected.reshape(tok_rows, head_count, HD)
    head_number = col_index * head_count + jnp.arange(head_count, dtype=jnp.int32)
    is_query = head_number < HEADS
    is_key = jnp.logical_and(head_number >= HEADS, head_number < HEADS + KV_HEADS)
    head_gain = jnp.where(is_query[:, None], q_gain[None, :], k_gain[None, :])
    head_scaled = normalize(per_head, head_gain)
    keep_norm = jnp.logical_or(is_query, is_key)[None, :, None]
    qkv_own = (
        jnp.where(keep_norm, head_scaled, per_head)
        .reshape(tok_rows, proj_width)
        .astype(jnp.bfloat16)
    )
    my_block = lax.axis_index("rep") * lax.axis_size("row") + lax.axis_index("row")
    from_peer = source // tok_rows != my_block
    local_row = source % tok_rows
    peer_resid, peer_qkv = swapped((resid_own, qkv_own), "rep", 0)
    picked = local_row + tok_rows * from_peer.astype(jnp.int32)
    moved_residual = jnp.take(jnp.concatenate([resid_own, peer_resid], axis=0), picked, axis=0)
    moved_qkv = jnp.take(jnp.concatenate([qkv_own, peer_qkv], axis=0), picked, axis=0)
    return (moved_residual, moved_qkv)


def solution(mesh):
    return jax.shard_map(
        per_device,
        mesh=mesh,
        in_specs=(
            P(("rep", "row"), "col"),
            P(),
            P("row", "col"),
            P("row", "col"),
            P("col", "row"),
            P(),
            P("row", "col"),
            P(),
            P(),
            P(("rep", "row")),
        ),
        out_specs=(P(("rep", "row"), "col"), P(("rep", "row"), "col")),
        check_vma=False,
    )
```

profile of v0, /device:TPU:1, one launch (start us, length us, event | category | flops | bytes accessed | tf_op | source)
XLA Modules:
  0.0 517.1 jit_solution(11629037548047053310)
XLA Ops:
  7.2 0.0 copy-start.7
  7.2 0.0 all-gather.7.cloned.1.call-start
  7.2 0.7 all-gather.7.cloned.1.call-update
  7.9 0.0 all-gather.9.cloned.1.call-start
  8.0 0.7 all-gather.9.cloned.1.call-update
  8.7 0.0 all-gather.11.cloned.1.call-start
  8.7 0.7 all-gather.11.cloned.1.call-update
  9.4 0.0 all-gather.13.cloned.1.call-start
  9.4 0.5 all-gather.13.cloned.1.call-update
  10.0 0.0 reduce-scatter.2.cloned.1.call-start
  10.0 74.2 %all-gather.7.cloned.1.call-done = bf16[512,2048]{1,0:T(8,128)(2,1)} async-done(((bf16[512,128]{1,0:T(8,128)(2,1)}), bf16[512,2048]{1,0:T(8,128)(2,1)}) %all-gather.7.cloned.1.call-update) | async-done | bytes 2097168 | tf_op jit(solution)/shard_map/all_gather | solution.py:26
  84.2 0.0 copy-start.1
  84.2 2.2 fusion
  86.4 65.4 %all-gather.9.cloned.1.call-done = bf16[2048,384]{1,0:T(8,128)(2,1)} async-done(((bf16[128,384]{1,0:T(8,128)(2,1)}), bf16[2048,384]{1,0:T(8,128)(2,1)}) %all-gather.9.cloned.1.call-update) | async-done | bytes 1572880 | tf_op jit(solution)/shard_map/all_gather | solution.py:32
  151.8 0.0 copy-done.7
  151.8 0.0 copy-done.1
  151.8 2.7 fusion.19
  154.5 59.1 %all-gather.11.cloned.1.call-done = bf16[2048,384]{1,0:T(8,128)(2,1)} async-done(((bf16[128,384]{1,0:T(8,128)(2,1)}), bf16[2048,384]{1,0:T(8,128)(2,1)}) %all-gather.11.cloned.1.call-update) | async-done | bytes 1572880 | tf_op jit(solution)/shard_map/all_gather | solution.py:36
  213.6 62.7 %all-gather.13.cloned.1.call-done = bf16[384,2048]{1,0:T(8,128)(2,1)} async-done(((bf16[384,128]{1,0:T(8,128)(2,1)}), bf16[384,2048]{1,0:T(8,128)(2,1)}) %all-gather.13.cloned.1.call-update) | async-done | bytes 1572880 | tf_op jit(solution)/shard_map/all_gather | solution.py:41
  276.3 6.2 %fusion.11 = f32[512,2048]{1,0:T(8,128)} fusion(bf16[384,2048]{1,0:T(8,128)(2,1)} %all-gather.13.cloned.1.call-done, bf16[2048,384]{1,0:T(8,128)(2,1)} %all-gather.11.cloned.1.call-done, f32[512,384]{1,0:T(8,128)S(1)} %fusion.19, bf16[512,2048]{1,0:T(8,128)(2,1)S(1)} %copy-done.1, f32[2048]{0:T(1024)S(1)} %copy-done.7, f32[512]{0:T(512)S(1)} %add_rsqrt_fusion.2), kind=kOutput, calls=%fused_computation.17 | convolution fusion | flops 1615986688 | bytes 10233856 | tf_op jit(solution)/shard_map/dot_general | solution.py:39
  282.5 0.0 copy-start.3
  282.6 0.0 copy-start.4
  282.6 0.0 copy-start.5
  282.6 0.0 copy-start.6
  282.6 0.0 reduce-scatter.2.cloned.1.call-update
  282.6 0.0 copy-start.8
  282.6 0.0 all-gather.15.cloned.1.call-start
  282.6 71.0 %reduce-scatter.2.cloned.1.call-done = f32[512,128]{1,0:T(8,128)} async-done(((f32[512,2048]{1,0:T(8,128)}), f32[512,128]{1,0:T(8,128)}) %reduce-scatter.2.cloned.1.call-update) | async-done | bytes 262160 | tf_op jit(solution)/shard_map/reduce_scatter | solution.py:44
  353.6 0.0 copy-done.3
  353.6 1.6 add_convert_fusion
  355.3 0.0 all-gather.15.cloned.1.call-update
  355.3 0.0 all-gather.17.cloned.1.call-start
  355.3 0.7 all-gather.17.cloned.1.call-update
  356.1 0.0 copy-done.4
  356.1 0.1 broadcast_bitcast_fusion
  356.2 0.0 copy-done.5
  356.2 0.0 copy-done.6
  356.2 0.1 bitcast_select_fusion
  356.3 11.9 %collective-permute-start = (bf16[512,128]{1,0:T(8,128)(2,1)}, bf16[512,128]{1,0:T(8,128)(2,1)S(1)}, u32[]{:S(2)}, u32[]{:S(2)}) collective-permute-start(bf16[512,128]{1,0:T(8,128)(2,1)} %add_convert_fusion), channel_id=1, source_target_pairs={{0,256},{256,0},{1,257},{257,1},{2,258},{258,2},{3,259},{259,3},{4... | collective-permute-start | bytes 393224 | tf_op jit(solution)/shard_map/ppermute | solution.py:15
  368.2 64.5 %all-gather.15.cloned.1.call-done = bf16[512,2048]{1,0:T(8,128)(2,1)} async-done(((bf16[512,128]{1,0:T(8,128)(2,1)}), bf16[512,2048]{1,0:T(8,128)(2,1)}) %all-gather.15.cloned.1.call-update) | async-done | bytes 2097168 | tf_op jit(solution)/shard_map/all_gather | solution.py:46
  432.6 0.0 copy-start
  432.6 2.2 fusion.3
  434.9 0.0 copy-start.2
  434.9 63.7 %all-gather.17.cloned.1.call-done = bf16[2048,256]{1,0:T(8,128)(2,1)} async-done(((bf16[128,256]{1,0:T(8,128)(2,1)}), bf16[2048,256]{1,0:T(8,128)(2,1)}) %all-gather.17.cloned.1.call-update) | async-done | bytes 1048592 | tf_op jit(solution)/shard_map/all_gather | solution.py:52
  498.6 0.0 copy-done.8
  498.6 0.0 copy-done
  498.6 2.2 bitcast_reduce_fusion
  500.8 0.1 fusion.23
  500.9 4.0 collective-permute-start.1
  504.9 0.0 collective-permute-done
  505.0 0.0 copy-done.2
  505.0 1.3 gather_fusion
  506.3 0.8 broadcast_select_fusion.1
  507.1 0.0 collective-permute-done.1
  507.1 0.1 pad_maximum_fusion
  507.2 0.2 copy.13
  507.4 2.0 gather_fusion.1
  509.4 0.8 broadcast_select_fusion
  (7 shorter events, 0.1 us)
Async XLA Ops:
  7.2 144.7 %copy-start.7 = (f32[2048]{0:T(1024)S(1)}, f32[2048]{0:T(1024)}, u32[]{:S(2)}) copy-start(f32[2048]{0:T(1024)} %param.11) | copy-start | bytes 24580
  7.2 77.0 %all-gather.7.cloned.1.call-start = ((), (), s32[]{:S(2)}) async-start(), calls=%async_computation.1 | async-start | bytes 2228224 | tf_op jit(solution)/shard_map/all_gather | solution.py:26
  7.9 143.9 %all-gather.9.cloned.1.call-start = ((), (), s32[]{:S(2)}) async-start(), calls=%async_computation.2 | async-start | bytes 1671168 | tf_op jit(solution)/shard_map/all_gather | solution.py:32
  8.7 204.9 %all-gather.11.cloned.1.call-start = ((), (), s32[]{:S(2)}) async-start(), calls=%async_computation.3 | async-start | bytes 1671168 | tf_op jit(solution)/shard_map/all_gather | solution.py:36
  9.4 266.9 %all-gather.13.cloned.1.call-start = ((), (), s32[]{:S(2)}) async-start(), calls=%async_computation.4 | async-start | bytes 1671168 | tf_op jit(solution)/shard_map/all_gather | solution.py:41
  10.0 343.7 %reduce-scatter.2.cloned.1.call-start = ((), (), s32[]{:S(2)}) async-start(), calls=%async_computation.5 | async-start | bytes 4456448 | tf_op jit(solution)/shard_map/reduce_scatter | solution.py:44
  84.2 67.6 %copy-start.1 = (bf16[512,2048]{1,0:T(8,128)(2,1)S(1)}, bf16[512,2048]{1,0:T(8,128)(2,1)}, u32[]{:S(2)}) copy-start(bf16[512,2048]{1,0:T(8,128)(2,1)} %all-gather.7.cloned.1.call-done) | copy-start | bytes 6291460
  282.5 71.1 %copy-start.3 = (bf16[512,128]{1,0:T(8,128)(2,1)S(1)}, bf16[512,128]{1,0:T(8,128)(2,1)}, u32[]{:S(2)}) copy-start(bf16[512,128]{1,0:T(8,128)(2,1)} %param.10) | copy-start | bytes 393220
  282.6 73.5 %copy-start.4 = (s32[512]{0:T(512)S(1)}, s32[512]{0:T(512)}, u32[]{:S(2)}) copy-start(s32[512]{0:T(512)} %param.19) | copy-start | bytes 6148
  282.6 73.6 %copy-start.5 = (f32[128]{0:T(128)S(1)}, f32[128]{0:T(128)}, u32[]{:S(2)}) copy-start(f32[128]{0:T(128)} %param.18) | copy-start | bytes 1540
  282.6 73.6 %copy-start.6 = (f32[128]{0:T(128)S(1)}, f32[128]{0:T(128)}, u32[]{:S(2)}) copy-start(f32[128]{0:T(128)} %param.17) | copy-start | bytes 1540
  282.6 216.0 %copy-start.8 = (f32[2048]{0:T(1024)S(1)}, f32[2048]{0:T(1024)}, u32[]{:S(2)}) copy-start(f32[2048]{0:T(1024)} %param.15) | copy-start | bytes 24580
  282.6 150.0 %all-gather.15.cloned.1.call-start = ((), (), s32[]{:S(2)}) async-start(), calls=%async_computation.6 | async-start | bytes 2228224 | tf_op jit(solution)/shard_map/all_gather | solution.py:46
  355.3 143.3 %all-gather.17.cloned.1.call-start = ((), (), s32[]{:S(2)}) async-start(), calls=%async_computation.7 | async-start | bytes 1114112 | tf_op jit(solution)/shard_map/all_gather | solution.py:52
  356.3 148.7 %collective-permute-start = (bf16[512,128]{1,0:T(8,128)(2,1)}, bf16[512,128]{1,0:T(8,128)(2,1)S(1)}, u32[]{:S(2)}, u32[]{:S(2)}) collective-permute-start(bf16[512,128]{1,0:T(8,128)(2,1)} %add_convert_fusion), channel_id=1, source_target_pairs={{0,256},{256,0},{1,257},{257,1},{2,258},{258,2},{3,259},{259,3},{4... | collective-permute-start | bytes 393224 | tf_op jit(solution)/shard_map/ppermute | solution.py:15
  432.6 65.9 %copy-start = (bf16[512,2048]{1,0:T(8,128)(2,1)S(1)}, bf16[512,2048]{1,0:T(8,128)(2,1)}, u32[]{:S(2)}) copy-start(bf16[512,2048]{1,0:T(8,128)(2,1)} %all-gather.15.cloned.1.call-done) | copy-start | bytes 6291460
  434.9 70.1 %copy-start.2 = (bf16[512,128]{1,0:T(8,128)(2,1)S(1)}, bf16[512,128]{1,0:T(8,128)(2,1)}, u32[]{:S(2)}) copy-start(bf16[512,128]{1,0:T(8,128)(2,1)} %add_convert_fusion) | copy-start | bytes 393220
  500.9 6.2 %collective-permute-start.1 = (bf16[512,256]{0,1:T(8,128)(2,1)S(1)}, bf16[512,256]{0,1:T(8,128)(2,1)S(1)}, u32[]{:S(2)}, u32[]{:S(2)}) collective-permute-start(bf16[512,256]{0,1:T(8,128)(2,1)S(1)} %fusion.23), channel_id=1, source_target_pairs={{0,256},{256,0},{1,257},{257,1},{2,258},{258,2},{3,259},{259,3},{4... | collective-permute-start | bytes 786440 | tf_op jit(solution)/shard_map/ppermute | solution.py:15
Sparse Core Ops, SparseCore 0:
  10.0 74.1 all-gather.6
  87.2 64.5 all-gather.8
  154.8 58.7 all-gather.10
  216.4 59.8 all-gather.12
  282.7 70.8 reduce-scatter.1
  356.1 76.5 all-gather.14
  435.7 62.8 all-gather.16
where the time goes:
time: 517 us
  waiting for transfers between devices  464 us (90%)
  starting transfers between devices  16.2 us (3%)
  between operations  14.3 us (3%)
  matrix products  11.1 us (2%)
  other arithmetic  8.07 us (2%)
    all_gather x1, waiting for transfers between devices, per_device(): gathered = lax.all_gather(residual, 'col', axis=1, tiled=True)  74.2 us
    reduce_scatter x1, waiting for transfers between devices, per_device(): lax.psum_scatter(partial_value, 'col', scatter_dimension=1, tiled=True)  71 us
    all_gather x1, waiting for transfers between devices, per_device(): lax.all_gather(w_gate, 'row', axis=0, tiled=True)  65.4 us
    all_gather x1, waiting for transfers between devices, per_device(): resid_full = lax.all_gather(resid_own, 'col', axis=1, tiled=True)  64.5 us
    all_gather x1, waiting for transfers between devices, per_device(): lax.all_gather(w_qkv, 'row', axis=0, tiled=True)  63.7 us
    all_gather x1, waiting for transfers between devices, per_device(): lax.all_gather(w_down, 'row', axis=1, tiled=True)  62.7 us
    all_gather x1, waiting for transfers between devices, per_device(): lax.all_gather(w_up, 'row', axis=0, tiled=True)  59.1 us
    ppermute x2, starting transfers between devices, swapped(): lax.ppermute(x, axis, [(i, i ^ 1 << apart) for i in range(lax.axis_size(a...  15.9 us
  transfers between devices with their start and end apart: 9, of which 7 were waited for; matrix products, arithmetic and copies ran while one was open for 2% of the time, Pallas kernels for 0%

commit v1 on v0

v1 whole, which is shorter than its diff:
```python
import functools

import jax
import jax.numpy as jnp
from jax import lax
from jax.experimental import pallas as pl
from jax.experimental.pallas import tpu as pltpu
from jax.sharding import PartitionSpec as P

HEADS = 16
KV_HEADS = 8
HD = 128
NX = 4
CHUNKS = 4
MESH = pl.DeviceIdType.MESH
F32 = jnp.float32
BF16 = jnp.bfloat16

epsilon = 1e-06


def step_kernel(
    n, nrow,
    res_ref, pg_ref, wg_ref, wu_ref, wd_ref, ng_ref, wq_ref, qg_ref, kg_ref, src_ref,
    out_r, out_q,
    x, x2, wgu, wdn, wqk, part, ring, first, hidden, onehot, rv, qv,
    a_send, a_recv, r_send, r_recv, b_send, b_recv,
    w_own, w1_send, w1_recv, w2_send, w2_recv, w3_send, w3_recv, p_send, p_recv,
):
    tok, feat = res_ref.shape
    ff = wg_ref.shape[1]
    qkw = wq_ref.shape[1]
    ny = nrow // NX
    ch = tok // CHUNKS
    tm = tok // 2
    width = n * feat
    me = lax.axis_index("col")
    rep = lax.axis_index("rep")
    row = lax.axis_index("row")
    py, px = row // NX, row % NX

    def ahead(k):
        return lax.rem(me + (k + 2 * n), n)

    right, left = ahead(1), ahead(-1)

    def rcopy(src, dst, ssem, rsem, **device):
        return pltpu.make_async_remote_copy(
            src_ref=src, dst_ref=dst, send_sem=ssem, recv_sem=rsem,
            device_id=device, device_id_type=MESH,
        )

    def x_peer(j):
        return py * NX + lax.rem(px + j, NX)

    def y_peer(j):
        return lax.rem(py + j, ny) * NX + px

    barrier = pltpu.get_barrier_semaphore()
    greeted = [dict(col=right), dict(col=left), dict(rep=1 - rep)]
    greeted += [dict(row=x_peer(j)) for j in range(1, NX)]
    greeted += [dict(row=y_peer(j)) for j in range(1, ny)]
    for device in greeted:
        pl.semaphore_signal(barrier, inc=1, device_id=device, device_id_type=MESH)
    pl.semaphore_wait(barrier, len(greeted))

    def hops(d, k):
        return n // 2 - (1 if (k >= CHUNKS // 2) == (d == 0) else 0)

    chains = [(d, k) for k in range(CHUNKS) for d in range(2)]
    most = n // 2

    def rows_of(k):
        return pl.ds(k * ch, ch)

    def gather_hop(buf, send, recv, d, k, s):
        blk = buf.at[ahead(-s if d == 0 else s), rows_of(k)]
        return rcopy(blk, blk, send.at[d, s, k], recv.at[d, s, k], col=right if d == 0 else left)

    def gather_arrival(buf, send, recv, d, k, s):
        blk = buf.at[ahead(-1 - s if d == 0 else 1 + s), rows_of(k)]
        return rcopy(blk, blk, send.at[d, s, k], recv.at[d, s, k], col=right if d == 0 else left)

    def gather_steps(buf, send, recv, lo, hi):
        def body(s, carry):
            for d, k in chains:
                gather_arrival(buf, send, recv, d, k, s).wait_recv()
                gather_hop(buf, send, recv, d, k, s + 1).start()
            return carry

        lax.fori_loop(lo, hi, body, 0)

    def gather_tail(buf, send, recv):
        for d, k in chains:
            gather_arrival(buf, send, recv, d, k, most - 2).wait_recv()
            if hops(d, k) == most:
                gather_hop(buf, send, recv, d, k, most - 1).start()
        for d, k in chains:
            if hops(d, k) == most:
                gather_arrival(buf, send, recv, d, k, most - 1).wait_recv()

    def drain(make, ):
        def body(s, carry):
            for d, k in chains:
                make(d, k, s).wait_send()
            return carry

        lax.fori_loop(0, most - 1, body, 0)
        for d, k in chains:
            if hops(d, k) == most:
                make(d, k, most - 1).wait_send()

    half_ff, half_q = ff // 2, qkw // 2

    def own_part(c, a):
        if a == 0:
            return wg_ref if c == 0 else wu_ref
        if a == 1:
            return wd_ref.at[pl.ds(c * half_ff, half_ff), :]
        return wq_ref.at[:, pl.ds(c * half_q, half_q)]

    def slot(c, a, y, q):
        lanes = pl.ds(pl.multiple_of(q * feat, feat), feat)
        if a == 0:
            return wgu.at[c, y, lanes, :]
        if a == 1:
            return wdn.at[y, pl.ds(c * half_ff, half_ff), lanes]
        return wqk.at[y, lanes, pl.ds(c * half_q, half_q)]

    def group(c, a, i):
        lanes = pl.ds(pl.multiple_of(i * feat, feat), feat)
        if a == 0:
            return wgu.at[0, i] if c == 0 else wgu.at[1, :, lanes, :]
        if a == 1:
            if c == 0:
                return wdn.at[i, pl.ds(0, half_ff), :]
            return wdn.at[:, pl.ds(half_ff, half_ff), lanes]
        if c == 0:
            return wqk.at[i, :, pl.ds(0, half_q)]
        return wqk.at[:, lanes, pl.ds(half_q, half_q)]

    def w_first(c, a, j):
        peer = x_peer(j) if c == 0 else y_peer(j)
        return rcopy(own_part(c, a), slot(c, a, py, px), w1_send.at[a, j - 1], w1_recv.at[a, j - 1], row=peer)

    def w_first_arrival(c, a, j):
        where = (py, lax.rem(px + NX - j, NX)) if c == 0 else (lax.rem(py + ny - j, ny), px)
        peer = x_peer(j) if c == 0 else y_peer(j)
        return rcopy(own_part(c, a), slot(c, a, *where), w1_send.at[a, j - 1], w1_recv.at[a, j - 1], row=peer)

    def w_local(c, a):
        return pltpu.make_async_copy(own_part(c, a), slot(c, a, py, px), w_own.at[a])

    def w_second(c, a, j):
        blk = group(c, a, py if c == 0 else px)
        peer = y_peer(j) if c == 0 else x_peer(j)
        return rcopy(blk, blk, w2_send.at[a, j - 1], w2_recv.at[a, j - 1], row=peer)

    def w_line(c, j):
        return lax.rem(py + ny - j, ny) if c == 0 else lax.rem(px + NX - j, NX)

    def w_second_arrival(c, a, j):
        blk = group(c, a, w_line(c, j))
        peer = y_peer(j) if c == 0 else x_peer(j)
        return rcopy(blk, blk, w2_send.at[a, j - 1], w2_recv.at[a, j - 1], row=peer)

    def w_relay(c, a, j):
        blk = group(c, a, w_line(c, j))
        return rcopy(blk, blk, w3_send.at[a, j], w3_recv.at[a, j], rep=1 - rep)

    def per_core(run):
        for c in range(2):
            pl.when(rep == c)(functools.partial(run, c))

    def stage_one(arrays):
        def run(c):
            for a in arrays:
                w_local(c, a).start()
                for j in range(1, 4):
                    w_first(c, a, j).start()

        per_core(run)

    def stage_two(arrays):
        def run(c):
            for a in arrays:
                w_local(c, a).wait()
                for j in range(1, 4):
                    w_first_arrival(c, a, j).wait_recv()
                for j in range(1, 4):
                    w_second(c, a, j).start()
                w_relay(c, a, 0).start()

        per_core(run)

    def stage_three(arrays):
        def run(c):
            for a in arrays:
                for j in range(1, 4):
                    w_second_arrival(c, a, j).wait_recv()
                    w_relay(c, a, j).start()

        per_core(run)

    def weights_here(arrays):
        def run(c):
            for a in arrays:
                for j in range(4):
                    w_relay(1 - c, a, j).wait_recv()

        per_core(run)

    def weights_sent(arrays):
        def run(c):
            for a in arrays:
                for j in range(1, 4):
                    w_first(c, a, j).wait_send()
                    w_second(c, a, j).wait_send()
                for j in range(4):
                    w_relay(c, a, j).wait_send()

        per_core(run)

    x[me] = res_ref[...]
    for d, k in chains:
        gather_hop(x, a_send, a_recv, d, k, 0).start()
    stage_one((0, 1))
    gather_steps(x, a_send, a_recv, 0, 1)
    stage_two((0, 1))

    mine = (rep * nrow + row) * tok
    other = ((1 - rep) * nrow + row) * tok
    for k in range(tok // HD):
        line = src_ref[k : k + 1, :]
        own = jnp.logical_and(line >= mine, line < mine + tok)
        place = jnp.where(own, line - mine, line - other + tok)
        down = jnp.transpose(jnp.broadcast_to(place, (HD, HD)))
        for b in range(2 * tok // HD):
            lane = lax.broadcasted_iota(jnp.int32, (HD, HD), 1) + b * HD
            onehot[pl.ds(k * HD, HD), pl.ds(b * HD, HD)] = jnp.where(down == lane, 1.0, 0.0).astype(BF16)

    gather_steps(x, a_send, a_recv, 1, most - 2)
    stage_three((0, 1))
    gather_tail(x, a_send, a_recv)
    weights_here((0, 1))

    def sum_first(d, k):
        to = ahead(hops(d, k) if d == 0 else -hops(d, k))
        return to, rcopy(
            first.at[d, k], ring.at[d, 0, k], r_send.at[d, 0, k], r_recv.at[d, 0, k],
            col=right if d == 0 else left,
        )

    def sum_hop(d, k, s):
        if isinstance(s, int) and s == 0:
            return sum_first(d, k)[1]
        return rcopy(
            ring.at[d, s - 1, k], ring.at[d, s, k], r_send.at[d, s, k], r_recv.at[d, s, k],
            col=right if d == 0 else left,
        )

    def sum_arrival(d, k, s):
        return rcopy(
            ring.at[d, s, k], ring.at[d, s, k], r_send.at[d, s, k], r_recv.at[d, s, k],
            col=right if d == 0 else left,
        )

    def scaled(buf, start, count, gain_ref):
        parts = [buf[b, pl.ds(start, count), :].astype(F32) for b in range(n)]
        total = parts[0] * parts[0]
        for p in parts[1:]:
            total = total + p * p
        scale = lax.rsqrt(jnp.sum(total, axis=-1, keepdims=True) / width + epsilon)
        return jnp.concatenate(
            [(p * scale * gain_ref[:, b * feat : (b + 1) * feat]).astype(BF16) for b, p in enumerate(parts)],
            axis=1,
        )

    for h in range(tok // tm):
        normed = scaled(x, h * tm, tm, pg_ref)
        gate = jnp.dot(normed, wgu[0].reshape(width, ff), preferred_element_type=F32)
        up = jnp.dot(normed, wgu[1].reshape(width, ff), preferred_element_type=F32)
        hidden[...] = (gate / (1.0 + jnp.exp(-gate)) * up).astype(BF16)
        for y in range(ny):
            value = jnp.dot(hidden[...], wdn[y], preferred_element_type=F32)
            for q in range(NX):
                part[y * NX + q, pl.ds(h * tm, tm), :] = value[:, q * feat : (q + 1) * feat]
        for d, k in chains:
            if h * tm <= k * ch < (h + 1) * tm:
                to, copy = sum_first(d, k)
                first[d, k] = part[to, rows_of(k), :].astype(BF16)
                copy.start()
    stage_one((2,))

    def sum_forward(d, k, s):
        sum_arrival(d, k, s - 1).wait_recv()
        to = ahead(hops(d, k) - s if d == 0 else s - hops(d, k))
        ring[d, s - 1, k] = (ring[d, s - 1, k].astype(F32) + part[to, rows_of(k), :]).astype(BF16)
        sum_hop(d, k, s).start()

    def sum_steps(lo, hi):
        def body(s, carry):
            for d, k in chains:
                sum_forward(d, k, s)
            return carry

        lax.fori_loop(lo, hi, body, 0)

    sum_steps(1, 3)
    stage_two((2,))
    sum_steps(3, most - 1)
    for d, k in chains:
        if hops(d, k) == most:
            sum_forward(d, k, most - 1)

    def resid_copy(k):
        return rcopy(
            rv.at[0, rows_of(k)], rv.at[1, rows_of(k)], p_send.at[0, k], p_recv.at[0, k], rep=1 - rep
        )

    def qkv_copy(k):
        return rcopy(
            qv.at[0, rows_of(k)], qv.at[1, rows_of(k)], p_send.at[1, k], p_recv.at[1, k], rep=1 - rep
        )

    for k in range(CHUNKS):
        total = part[me, rows_of(k), :]
        for d in range(2):
            last = hops(d, k) - 1
            sum_arrival(d, k, last).wait_recv()
            total = total + ring[d, last, k].astype(F32)
        fresh = (res_ref[rows_of(k), :].astype(F32) + total).astype(BF16)
        x2[me, rows_of(k), :] = fresh
        rv[0, rows_of(k), :] = fresh
        for d in range(2):
            gather_hop(x2, b_send, b_recv, d, k, 0).start()
        resid_copy(k).start()

    stage_three((2,))
    gather_steps(x2, b_send, b_recv, 0, most - 3)
    for k in range(CHUNKS):
        resid_copy(k).wait_recv()
    out_r[...] = (
        jnp.dot(onehot[:, :tok], rv[0], preferred_element_type=F32)
        + jnp.dot(onehot[:, tok:], rv[1], preferred_element_type=F32)
    ).astype(BF16)
    gather_steps(x2, b_send, b_recv, most - 3, most - 2)
    gather_tail(x2, b_send, b_recv)
    weights_here((2,))

    for h in range(tok // tm):
        normed = scaled(x2, h * tm, tm, ng_ref)
        projected = jnp.dot(normed, wqk[...].reshape(width, qkw), preferred_element_type=F32)
        for i in range(qkw // HD):
            head = me * (qkw // HD) + i
            value = projected[:, i * HD : (i + 1) * HD]
            scale = lax.rsqrt(jnp.mean(value * value, axis=-1, keepdims=True) + epsilon)
            gain = jnp.where(jnp.full((1, HD), head, jnp.int32) < HEADS, qg_ref[...], kg_ref[...])
            normal = jnp.full((tm, HD), head, jnp.int32) < HEADS + KV_HEADS
            qv[0, pl.ds(h * tm, tm), i * HD : (i + 1) * HD] = jnp.where(
                normal, value * scale * gain, value
            ).astype(BF16)
        for k in range(CHUNKS):
            if h * tm <= k * ch < (h + 1) * tm:
                qkv_copy(k).start()

    drain(lambda d, k, s: gather_hop(x, a_send, a_recv, d, k, s))
    drain(lambda d, k, s: rcopy(
        ring.at[d, s, k], ring.at[d, s, k], r_send.at[d, s, k], r_recv.at[d, s, k],
        col=right if d == 0 else left,
    ))
    drain(lambda d, k, s: gather_hop(x2, b_send, b_recv, d, k, s))
    weights_sent((0, 1, 2))
    for k in range(CHUNKS):
        resid_copy(k).wait_send()
        qkv_copy(k).wait_send()
        qkv_copy(k).wait_recv()
    out_q[...] = (
        jnp.dot(onehot[:, :tok], qv[0], preferred_element_type=F32)
        + jnp.dot(onehot[:, tok:], qv[1], preferred_element_type=F32)
    ).astype(BF16)


def per_device(residual, post_gain, w_gate, w_up, w_down, next_gain, w_qkv, q_gain, k_gain, source):
    n = lax.axis_size("col")
    nrow = lax.axis_size("row")
    ny = nrow // NX
    tok, feat = residual.shape
    ff = w_gate.shape[1]
    qkw = w_qkv.shape[1]
    ch = tok // CHUNKS
    most = n // 2
    ring_sems = pltpu.SemaphoreType.DMA((2, most, CHUNKS))
    return pl.pallas_call(
        functools.partial(step_kernel, n, nrow),
        out_shape=(
            jax.ShapeDtypeStruct((tok, feat), BF16),
            jax.ShapeDtypeStruct((tok, qkw), BF16),
        ),
        in_specs=[pl.BlockSpec(memory_space=pltpu.VMEM)] * 10,
        out_specs=(pl.BlockSpec(memory_space=pltpu.VMEM),) * 2,
        scratch_shapes=[
            pltpu.VMEM((n, tok, feat), BF16),
            pltpu.VMEM((n, tok, feat), BF16),
            pltpu.VMEM((2, ny, NX * feat, ff), BF16),
            pltpu.VMEM((ny, ff, NX * feat), BF16),
            pltpu.VMEM((ny, NX * feat, qkw), BF16),
            pltpu.VMEM((n, tok, feat), F32),
            pltpu.VMEM((2, most, CHUNKS, ch, feat), BF16),
            pltpu.VMEM((2, CHUNKS, ch, feat), BF16),
            pltpu.VMEM((tok // 2, ff), BF16),
            pltpu.VMEM((tok, 2 * tok), BF16),
            pltpu.VMEM((2, tok, feat), BF16),
            pltpu.VMEM((2, tok, qkw), BF16),
            ring_sems, ring_sems, ring_sems, ring_sems, ring_sems, ring_sems,
            pltpu.SemaphoreType.DMA((3,)),
            pltpu.SemaphoreType.DMA((3, 3)),
            pltpu.SemaphoreType.DMA((3, 3)),
            pltpu.SemaphoreType.DMA((3, 3)),
            pltpu.SemaphoreType.DMA((3, 3)),
            pltpu.SemaphoreType.DMA((3, 4)),
            pltpu.SemaphoreType.DMA((3, 4)),
            pltpu.SemaphoreType.DMA((2, CHUNKS)),
            pltpu.SemaphoreType.DMA((2, CHUNKS)),
        ],
        compiler_params=pltpu.CompilerParams(
            collective_id=0, has_side_effects=True, vmem_limit_bytes=48 * 1024 * 1024
        ),
        name="block_step",
    )(
        residual, post_gain.reshape(1, -1), w_gate, w_up, w_down, next_gain.reshape(1, -1), w_qkv,
        q_gain.reshape(1, -1), k_gain.reshape(1, -1), source.reshape(-1, HD),
    )


def solution(mesh):
    return jax.shard_map(
        per_device,
        mesh=mesh,
        in_specs=(
            P(("rep", "row"), "col"),
            P(),
            P("row", "col"),
            P("row", "col"),
            P("col", "row"),
            P(),
            P("row", "col"),
            P(),
            P(),
            P(("rep", "row")),
        ),
        out_specs=(P(("rep", "row"), "col"), P(("rep", "row"), "col")),
        check_vma=False,
    )
```

time: 517 us -> 119 us (0.23)
  waiting for transfers between devices: 464 us -> 0 us
  Pallas kernels: 0 us -> 110 us
  starting transfers between devices: 16.2 us -> 0 us
  between operations: 14.3 us -> 0.67 us
  matrix products: 11.1 us -> 0 us
  other arithmetic: 8.07 us -> 0 us
    all_gather x6 -> x0, waiting for transfers between devices: 390 us -> none  [the longest x1 74.2 us: per_device(): gathered = lax.all_gather(residual, 'col', axis=1, tiled=True)]
    pallas_call x0 -> x1, Pallas kernels: none -> 110 us  [per_device(): pl.pallas_call(functools.partial(step_kernel, n, nrow), out_shape=(jax.Sh...]
    reduce_scatter x1 -> x0, waiting for transfers between devices: 71 us -> none  [per_device(): lax.psum_scatter(partial_value, 'col', scatter_dimension=1, tiled=True)]
    ppermute x2 -> x0, starting transfers between devices: 15.9 us -> none  [swapped(): lax.ppermute(x, axis, [(i, i ^ 1 << apart) for i in range(lax.axis_size(a...]
    dot_general x3 -> x0, matrix products: 11.1 us -> none  [the longest x1 6.24 us: per_device(): jnp.dot(hidden, lax.all_gather(w_down, 'row', axis=1, tiled=True), prefer...]
    unnamed x18 -> x22, local copies, waits for them, and re-layouts: 0.04 us -> 7.84 us
  transfers between devices with their start and end apart: 9 -> 0, of which waited for: 7 -> 0; matrix products, arithmetic and copies ran while one was open for 2% -> 0% of each run, Pallas kernels for 0% -> 0%
where the time goes in v1:
time: 119 us; the launch traced here: 118 us
  Pallas kernels  110 us (92%)
  local copies, waits for them, and re-layouts  7.84 us (7%)
    pallas_call x1, Pallas kernels, per_device(): pl.pallas_call(functools.partial(step_kernel, n, nrow), out_shape=(jax.Sh...  110 us
    unnamed x22, local copies, waits for them, and re-layouts  7.84 us

profile of v1, /device:TPU:1, one launch (start us, length us, event | category | flops | bytes accessed | tf_op | source)
XLA Modules:
  0.0 118.0 jit_solution(4962894025274010725)
XLA Ops:
  0.6 0.0 copy-start.5
  0.6 0.0 copy-start.8
  0.7 0.0 copy-start.9
  0.7 0.7 copy-done.5
  1.3 0.0 copy-done.8
  1.3 0.0 copy-done.9
  1.3 0.0 copy-start
  1.3 0.9 copy-done
  2.2 0.0 copy-start.1
  2.2 0.9 copy-done.1
  3.1 0.0 copy-start.2
  3.1 0.9 copy-done.2
  4.0 0.0 copy-start.3
  4.0 0.9 copy-done.3
  4.9 0.0 copy-start.4
  4.9 0.8 copy-done.4
  5.8 0.0 copy-start.6
  5.8 0.7 copy-done.6
  6.5 0.0 copy-start.7
  6.5 0.7 copy-done.7
  7.1 109.5 %block_step.1 = (bf16[512,128]{1,0:T(8,128)(2,1)S(1)}, bf16[512,256]{1,0:T(8,128)(2,1)S(1)}) custom-call(bf16[512,128]{1,0:T(8,128)(2,1)S(1)} %copy-done, f32[1,2048]{1,0:T(1,128)S(1)} %bitcast.5, bf16[128,384]{1,0:T(8,128)(2,1)S(1)} %copy-done.1, bf16[128,384]{1,0:T(8,128)(2,1)S(1)} %copy-done.2, bf16[384,128]{1,0:T(8,128)(2,1)S(1)} %copy-done.3, ...), custom_call_target="tpu_custom_call" | custom-call | tf_op jit(solution)/shard_map/block_step/pallas_call | solution.py:394
  116.7 0.7 copy.14
  117.3 0.7 copy.15
Async XLA Ops:
  0.6 0.7 copy-start.5
  0.6 0.7 copy-start.8
  0.7 0.7 copy-start.9
  1.3 0.9 copy-start
  2.2 0.9 copy-start.1
  3.1 0.9 copy-start.2
  4.0 0.9 copy-start.3
  4.9 0.8 copy-start.4
  5.8 0.7 copy-start.6
  6.5 0.7 copy-start.7

commit v2 on v1

v2 whole, which is shorter than its diff:
```python
import functools

import jax
import jax.numpy as jnp
from jax import lax
from jax.experimental import pallas as pl
from jax.experimental.pallas import tpu as pltpu
from jax.sharding import PartitionSpec as P

HEADS = 16
KV_HEADS = 8
HD = 128
NX = 4
CHUNKS = 4
MESH = pl.DeviceIdType.MESH
F32 = jnp.float32
BF16 = jnp.bfloat16

epsilon = 1e-06


def step_kernel(
    n, nrow,
    res_hbm, pg_hbm, wg_hbm, wu_hbm, wd_hbm, ng_hbm, wq_hbm, qg_hbm, kg_hbm, src_hbm,
    out_r, out_q,
    pg_ref, ng_ref, qg_ref, kg_ref, src_ref,
    x, x2, wgu, wdn, wqk, gated, squares, proj, part, ring, first, onehot, rv, qv,
    a_send, a_recv, r_send, r_recv, b_send, b_recv,
    small, w_own, w1_send, w1_recv, w2_send, w2_recv, w3_send, w3_recv, p_send, p_recv,
):
    tok, feat = res_hbm.shape
    ff = wg_hbm.shape[1]
    qkw = wq_hbm.shape[1]
    ny = nrow // NX
    ch = tok // CHUNKS
    tm = tok // 2
    width = n * feat
    me = lax.axis_index("col")
    rep = lax.axis_index("rep")
    row = lax.axis_index("row")
    py, px = row // NX, row % NX

    def ahead(k):
        return lax.rem(me + (k + 2 * n), n)

    right, left = ahead(1), ahead(-1)

    def rcopy(src, dst, ssem, rsem, **device):
        return pltpu.make_async_remote_copy(
            src_ref=src, dst_ref=dst, send_sem=ssem, recv_sem=rsem,
            device_id=device, device_id_type=MESH,
        )

    def x_peer(j):
        return py * NX + lax.rem(px + j, NX)

    def y_peer(j):
        return lax.rem(py + j, ny) * NX + px

    loads = [
        pltpu.make_async_copy(src, dst, small.at[i])
        for i, (src, dst) in enumerate((
            (res_hbm, x.at[me]), (src_hbm, src_ref), (pg_hbm, pg_ref),
            (ng_hbm, ng_ref), (qg_hbm, qg_ref), (kg_hbm, kg_ref),
        ))
    ]
    for load in loads:
        load.start()

    barrier = pltpu.get_barrier_semaphore()
    greeted = [dict(col=right), dict(col=left), dict(rep=1 - rep)]
    greeted += [dict(row=x_peer(j)) for j in range(1, NX)]
    greeted += [dict(row=y_peer(j)) for j in range(1, ny)]
    for device in greeted:
        pl.semaphore_signal(barrier, inc=1, device_id=device, device_id_type=MESH)
    pl.semaphore_wait(barrier, len(greeted))

    def hops(d, k):
        return n // 2 - (1 if (k >= CHUNKS // 2) == (d == 0) else 0)

    chains = [(d, k) for k in range(CHUNKS) for d in range(2)]
    most = n // 2
    halves = tok // tm

    def rows_of(k):
        return pl.ds(k * ch, ch)

    def in_half(h):
        return [(d, k) for d, k in chains if h * tm <= k * ch < (h + 1) * tm]

    def gather_hop(buf, send, recv, d, k, s):
        blk = buf.at[ahead(-s if d == 0 else s), rows_of(k)]
        return rcopy(blk, blk, send.at[d, s, k], recv.at[d, s, k], col=right if d == 0 else left)

    def gather_arrival(buf, send, recv, d, k, s):
        blk = buf.at[ahead(-1 - s if d == 0 else 1 + s), rows_of(k)]
        return rcopy(blk, blk, send.at[d, s, k], recv.at[d, s, k], col=right if d == 0 else left)

    def first_hop(d, k):
        return rcopy(
            res_hbm.at[rows_of(k)], x.at[me, rows_of(k)], a_send.at[d, 0, k], a_recv.at[d, 0, k],
            col=right if d == 0 else left,
        )

    def gather_step(buf, send, recv, s, group):
        for d, k in group:
            gather_arrival(buf, send, recv, d, k, s).wait_recv()
            if not isinstance(s, int) or s + 1 < hops(d, k):
                gather_hop(buf, send, recv, d, k, s + 1).start()

    def gather_steps(buf, send, recv, lo, hi, extra=None):
        def body(s, carry):
            gather_step(buf, send, recv, s, chains)
            if extra is not None:
                extra(s)
            return carry

        lax.fori_loop(lo, hi, body, 0)

    def last_arrivals(buf, send, recv, group):
        for d, k in group:
            if hops(d, k) == most:
                gather_arrival(buf, send, recv, d, k, most - 1).wait_recv()

    def sent(make, s):
        for d, k in chains:
            if not isinstance(s, int) or s < hops(d, k):
                make(d, k, s).wait_send()

    half_ff, half_q = ff // 2, qkw // 2

    def own_part(c, a):
        if a == 0:
            return wg_hbm if c == 0 else wu_hbm
        if a == 1:
            return wd_hbm.at[pl.ds(c * half_ff, half_ff), :]
        return wq_hbm.at[:, pl.ds(c * half_q, half_q)]

    def slot(c, a, y, q):
        if a == 0:
            return wgu.at[c, y, q]
        if a == 1:
            return wdn.at[y, pl.ds(c * half_ff, half_ff), pl.ds(pl.multiple_of(q * feat, feat), feat)]
        return wqk.at[y, q, :, pl.ds(c * half_q, half_q)]

    def group(c, a, i):
        if a == 0:
            return wgu.at[0, i] if c == 0 else wgu.at[1, :, i]
        if a == 1:
            if c == 0:
                return wdn.at[i, pl.ds(0, half_ff), :]
            return wdn.at[:, pl.ds(half_ff, half_ff), pl.ds(pl.multiple_of(i * feat, feat), feat)]
        if c == 0:
            return wqk.at[i, :, :, pl.ds(0, half_q)]
        return wqk.at[:, i, :, pl.ds(half_q, half_q)]

    def w_first(c, a, j):
        peer = x_peer(j) if c == 0 else y_peer(j)
        return rcopy(own_part(c, a), slot(c, a, py, px), w1_send.at[a, j - 1], w1_recv.at[a, j - 1], row=peer)

    def w_first_arrival(c, a, j):
        where = (py, lax.rem(px + NX - j, NX)) if c == 0 else (lax.rem(py + ny - j, ny), px)
        peer = x_peer(j) if c == 0 else y_peer(j)
        return rcopy(own_part(c, a), slot(c, a, *where), w1_send.at[a, j - 1], w1_recv.at[a, j - 1], row=peer)

    def w_local(c, a):
        return pltpu.make_async_copy(own_part(c, a), slot(c, a, py, px), w_own.at[a])

    def w_second(c, a, j):
        blk = group(c, a, py if c == 0 else px)
        peer = y_peer(j) if c == 0 else x_peer(j)
        return rcopy(blk, blk, w2_send.at[a, j - 1], w2_recv.at[a, j - 1], row=peer)

    def w_line(c, j):
        return lax.rem(py + ny - j, ny) if c == 0 else lax.rem(px + NX - j, NX)

    def w_second_arrival(c, a, j):
        blk = group(c, a, w_line(c, j))
        peer = y_peer(j) if c == 0 else x_peer(j)
        return rcopy(blk, blk, w2_send.at[a, j - 1], w2_recv.at[a, j - 1], row=peer)

    def w_relay(c, a, j):
        blk = group(c, a, w_line(c, j))
        return rcopy(blk, blk, w3_send.at[a, j], w3_recv.at[a, j], rep=1 - rep)

    def per_core(run):
        for c in range(2):
            pl.when(rep == c)(functools.partial(run, c))

    def stage_one(arrays):
        def run(c):
            for a in arrays:
                for j in range(1, 4):
                    w_first(c, a, j).start()
                w_local(c, a).start()

        per_core(run)

    def stage_two(arrays):
        def run(c):
            for a in arrays:
                w_local(c, a).wait()
                for j in range(1, 4):
                    w_first_arrival(c, a, j).wait_recv()
                for j in range(1, 4):
                    w_second(c, a, j).start()
                w_relay(c, a, 0).start()

        per_core(run)

    def stage_three(arrays):
        def run(c):
            for a in arrays:
                for j in range(1, 4):
                    w_second_arrival(c, a, j).wait_recv()
                    w_relay(c, a, j).start()

        per_core(run)

    def weights_here(arrays):
        def run(c):
            for a in arrays:
                for j in range(4):
                    w_relay(1 - c, a, j).wait_recv()

        per_core(run)

    def weights_sent(arrays):
        def run(c):
            for a in arrays:
                for j in range(1, 4):
                    w_first(c, a, j).wait_send()
                    w_second(c, a, j).wait_send()
                for j in range(4):
                    w_relay(c, a, j).wait_send()

        per_core(run)

    def pair(s):
        return [me, ahead(most)] if s is None else [ahead(-1 - s), ahead(1 + s)]

    def taken(buf, gain_ref, blocks, rows):
        values = [buf[b, rows, :].astype(F32) for b in blocks]
        square = values[0] * values[0]
        for v in values[1:]:
            square = square + v * v
        lhs = jnp.concatenate([(v * gain_ref[pl.ds(b, 1), :]).astype(BF16) for v, b in zip(values, blocks)], axis=1)
        return square, lhs

    def row_scale(square):
        return lax.rsqrt(jnp.sum(square, axis=-1, keepdims=True) / width + epsilon)

    def gate_up(h, steps, fresh):
        rows = pl.ds(h * tm, tm)
        blocks = [b for s in steps for b in pair(s)]
        square, lhs = taken(x, pg_ref, blocks, rows)
        both = []
        for c in range(2):
            rhs = jnp.concatenate([wgu[c, b // NX, lax.rem(b, NX)] for b in blocks], axis=0)
            both.append(jnp.dot(lhs, rhs, preferred_element_type=F32))
        if not fresh:
            square = square + squares[rows, :]
            both = [v + gated[c, rows, :] for c, v in enumerate(both)]
        return square, both

    def gate_up_add(h, steps, fresh):
        rows = pl.ds(h * tm, tm)
        square, both = gate_up(h, steps, fresh)
        squares[rows, :] = square
        for c in range(2):
            gated[c, rows, :] = both[c]

    stage_one((0,))
    for d, k in chains:
        first_hop(d, k).start()
    stage_one((1,))
    for load in loads:
        load.wait()
    gather_step(x, a_send, a_recv, 0, chains)
    stage_two((0,))
    gather_step(x, a_send, a_recv, 1, chains)
    stage_two((1,))

    mine = (rep * nrow + row) * tok
    other = ((1 - rep) * nrow + row) * tok

    def select_rows(k):
        line = src_ref[pl.ds(k, 1), :]
        own = jnp.logical_and(line >= mine, line < mine + tok)
        place = jnp.where(own, line - mine, line - other + tok)
        down = jnp.transpose(jnp.broadcast_to(place, (HD, HD)))
        for b in range(2 * tok // HD):
            lane = lax.broadcasted_iota(jnp.int32, (HD, HD), 1) + b * HD
            onehot[pl.ds(pl.multiple_of(k * HD, HD), HD), pl.ds(b * HD, HD)] = jnp.where(
                down == lane, 1.0, 0.0
            ).astype(BF16)

    gather_steps(x, a_send, a_recv, 2, most - 3)
    stage_three((0,))
    gather_step(x, a_send, a_recv, most - 3, chains)
    weights_here((0,))
    for h in range(halves):
        gate_up_add(h, (0, 1, 2), True)
    for h in range(halves):
        gather_step(x, a_send, a_recv, most - 2, in_half(h))
    stage_three((1,))
    for h in range(halves):
        gate_up_add(h, (3, 4, 5, 6), False)

    def sum_first(d, k):
        to = ahead(hops(d, k) if d == 0 else -hops(d, k))
        return to, rcopy(
            first.at[d, k], ring.at[d, 0, k], r_send.at[d, 0, k], r_recv.at[d, 0, k],
            col=right if d == 0 else left,
        )

    def sum_hop(d, k, s):
        return rcopy(
            ring.at[d, s - 1, k], ring.at[d, s, k], r_send.at[d, s, k], r_recv.at[d, s, k],
            col=right if d == 0 else left,
        )

    def sum_arrival(d, k, s):
        return rcopy(
            ring.at[d, s, k], ring.at[d, s, k], r_send.at[d, s, k], r_recv.at[d, s, k],
            col=right if d == 0 else left,
        )

    for h in range(halves):
        last_arrivals(x, a_send, a_recv, in_half(h))
        square, (gate, up) = gate_up(h, (None,), False)
        scale = row_scale(square)
        gate = gate * scale
        up = up * scale
        hidden = (gate / (1.0 + jnp.exp(-gate)) * up).astype(BF16)
        if h == 0:
            weights_here((1,))
        for y in range(ny):
            value = jnp.dot(hidden, wdn[y], preferred_element_type=F32)
            for q in range(NX):
                part[y * NX + q, pl.ds(h * tm, tm), :] = value[:, q * feat : (q + 1) * feat]
        for d, k in in_half(h):
            to, copy = sum_first(d, k)
            first[d, k] = part[to, rows_of(k), :].astype(BF16)
            copy.start()
    stage_one((2,))

    def sum_forward(d, k, s):
        sum_arrival(d, k, s - 1).wait_recv()
        to = ahead(hops(d, k) - s if d == 0 else s - hops(d, k))
        ring[d, s - 1, k] = (ring[d, s - 1, k].astype(F32) + part[to, rows_of(k), :]).astype(BF16)
        sum_hop(d, k, s).start()

    def a_hop(d, k, s):
        return gather_hop(x, a_send, a_recv, d, k, s)

    def sum_steps(lo, hi):
        def body(s, carry):
            for d, k in chains:
                sum_forward(d, k, s)
            sent(a_hop, s - 1)
            return carry

        lax.fori_loop(lo, hi, body, 0)

    sum_steps(1, 3)
    stage_two((2,))
    sum_steps(3, most - 1)
    for k in range(tok // HD):
        select_rows(k)
    for d, k in chains:
        if hops(d, k) == most:
            sum_forward(d, k, most - 1)
    sent(a_hop, most - 2)
    sent(a_hop, most - 1)

    def resid_copy(k):
        return rcopy(
            rv.at[0, rows_of(k)], rv.at[1, rows_of(k)], p_send.at[0, k], p_recv.at[0, k], rep=1 - rep
        )

    def qkv_copy(k):
        return rcopy(
            qv.at[0, rows_of(k)], qv.at[1, rows_of(k)], p_send.at[1, k], p_recv.at[1, k], rep=1 - rep
        )

    for k in range(CHUNKS):
        total = part[me, rows_of(k), :]
        for d in range(2):
            last = hops(d, k) - 1
            sum_arrival(d, k, last).wait_recv()
            total = total + ring[d, last, k].astype(F32)
        fresh = (x[me, rows_of(k), :].astype(F32) + total).astype(BF16)
        x2[me, rows_of(k), :] = fresh
        rv[0, rows_of(k), :] = fresh
        for d in range(2):
            gather_hop(x2, b_send, b_recv, d, k, 0).start()
        resid_copy(k).start()

    stage_three((2,))

    def qkv_part(rows, s, fresh):
        blocks = pair(s)
        square, lhs = taken(x2, ng_ref, blocks, rows)
        rhs = jnp.concatenate([wqk[b // NX, lax.rem(b, NX)] for b in blocks], axis=0)
        value = jnp.dot(lhs, rhs, preferred_element_type=F32)
        if not fresh:
            square = square + squares[rows, :]
            value = value + proj[rows, :]
        return square, value

    def qkv_add(s, fresh):
        for h in range(halves):
            rows = pl.ds(h * tm, tm)
            square, value = qkv_part(rows, s, fresh)
            squares[rows, :] = square
            proj[rows, :] = value

    def b_hop(d, k, s):
        return gather_hop(x2, b_send, b_recv, d, k, s)

    gather_step(x2, b_send, b_recv, 0, chains)
    weights_here((2,))
    qkv_add(0, True)
    sent(sum_arrival, 0)
    weights_sent((0, 1, 2))

    def later(s):
        qkv_add(s, False)
        sent(sum_arrival, s)
        sent(b_hop, s - 1)

    gather_steps(x2, b_send, b_recv, 1, most - 3, later)
    for k in range(CHUNKS):
        resid_copy(k).wait_recv()
    out_r[...] = (
        jnp.dot(onehot[:, :tok], rv[0], preferred_element_type=F32)
        + jnp.dot(onehot[:, tok:], rv[1], preferred_element_type=F32)
    ).astype(BF16)
    gather_steps(x2, b_send, b_recv, most - 3, most - 2, later)
    gather_step(x2, b_send, b_recv, most - 2, chains)
    qkv_add(most - 2, False)
    sent(sum_arrival, most - 2)
    sent(sum_arrival, most - 1)
    sent(b_hop, most - 3)

    for h in range(halves):
        last_arrivals(x2, b_send, b_recv, in_half(h))
        rows = pl.ds(h * tm, tm)
        square, projected = qkv_part(rows, None, False)
        projected = projected * row_scale(square)
        for i in range(qkw // HD):
            head = me * (qkw // HD) + i
            value = projected[:, i * HD : (i + 1) * HD]
            scale = lax.rsqrt(jnp.mean(value * value, axis=-1, keepdims=True) + epsilon)
            gain = jnp.where(jnp.full((1, HD), head, jnp.int32) < HEADS, qg_ref[...], kg_ref[...])
            normal = jnp.full((tm, HD), head, jnp.int32) < HEADS + KV_HEADS
            qv[0, rows, i * HD : (i + 1) * HD] = jnp.where(normal, value * scale * gain, value).astype(BF16)
        for k in range(CHUNKS):
            if h * tm <= k * ch < (h + 1) * tm:
                qkv_copy(k).start()

    own_rows = jnp.dot(onehot[:, :tok], qv[0], preferred_element_type=F32)
    sent(b_hop, most - 2)
    sent(b_hop, most - 1)
    for k in range(CHUNKS):
        resid_copy(k).wait_send()
        qkv_copy(k).wait_send()
        qkv_copy(k).wait_recv()
    out_q[...] = (own_rows + jnp.dot(onehot[:, tok:], qv[1], preferred_element_type=F32)).astype(BF16)


def per_device(residual, post_gain, w_gate, w_up, w_down, next_gain, w_qkv, q_gain, k_gain, source):
    n = lax.axis_size("col")
    nrow = lax.axis_size("row")
    ny = nrow // NX
    tok, feat = residual.shape
    ff = w_gate.shape[1]
    qkw = w_qkv.shape[1]
    ch = tok // CHUNKS
    most = n // 2
    ring_sems = pltpu.SemaphoreType.DMA((2, most, CHUNKS))
    return pl.pallas_call(
        functools.partial(step_kernel, n, nrow),
        out_shape=(
            jax.ShapeDtypeStruct((tok, feat), BF16),
            jax.ShapeDtypeStruct((tok, qkw), BF16),
        ),
        in_specs=[pl.BlockSpec(memory_space=pl.ANY)] * 10,
        out_specs=(pl.BlockSpec(memory_space=pltpu.VMEM),) * 2,
        scratch_shapes=[
            pltpu.VMEM((n, feat), F32),
            pltpu.VMEM((n, feat), F32),
            pltpu.VMEM((1, HD), F32),
            pltpu.VMEM((1, HD), F32),
            pltpu.VMEM((tok // HD, HD), jnp.int32),
            pltpu.VMEM((n, tok, feat), BF16),
            pltpu.VMEM((n, tok, feat), BF16),
            pltpu.VMEM((2, ny, NX, feat, ff), BF16),
            pltpu.VMEM((ny, ff, NX * feat), BF16),
            pltpu.VMEM((ny, NX, feat, qkw), BF16),
            pltpu.VMEM((2, tok, ff), F32),
            pltpu.VMEM((tok, feat), F32),
            pltpu.VMEM((tok, qkw), F32),
            pltpu.VMEM((n, tok, feat), F32),
            pltpu.VMEM((2, most, CHUNKS, ch, feat), BF16),
            pltpu.VMEM((2, CHUNKS, ch, feat), BF16),
            pltpu.VMEM((tok, 2 * tok), BF16),
            pltpu.VMEM((2, tok, feat), BF16),
            pltpu.VMEM((2, tok, qkw), BF16),
            ring_sems, ring_sems, ring_sems, ring_sems, ring_sems, ring_sems,
            pltpu.SemaphoreType.DMA((6,)),
            pltpu.SemaphoreType.DMA((3,)),
            pltpu.SemaphoreType.DMA((3, 3)),
            pltpu.SemaphoreType.DMA((3, 3)),
            pltpu.SemaphoreType.DMA((3, 3)),
            pltpu.SemaphoreType.DMA((3, 3)),
            pltpu.SemaphoreType.DMA((3, 4)),
            pltpu.SemaphoreType.DMA((3, 4)),
            pltpu.SemaphoreType.DMA((2, CHUNKS)),
            pltpu.SemaphoreType.DMA((2, CHUNKS)),
        ],
        compiler_params=pltpu.CompilerParams(
            collective_id=0, has_side_effects=True, vmem_limit_bytes=60 * 1024 * 1024
        ),
        name="block_step",
    )(
        residual, post_gain.reshape(n, feat), w_gate, w_up, w_down, next_gain.reshape(n, feat), w_qkv,
        q_gain.reshape(1, -1), k_gain.reshape(1, -1), source.reshape(-1, HD),
    )


def solution(mesh):
    return jax.shard_map(
        per_device,
        mesh=mesh,
        in_specs=(
            P(("rep", "row"), "col"),
            P(),
            P("row", "col"),
            P("row", "col"),
            P("col", "row"),
            P(),
            P("row", "col"),
            P(),
            P(),
            P(("rep", "row")),
        ),
        out_specs=(P(("rep", "row"), "col"), P(("rep", "row"), "col")),
        check_vma=False,
    )
```

time: 119 us -> 108 us (0.908)
  local copies, waits for them, and re-layouts: 7.84 us -> 2.32 us
  Pallas kernels: 110 us -> 105 us
    unnamed x22 -> x4, local copies, waits for them, and re-layouts: 7.84 us -> 2.32 us
    pallas_call x1, Pallas kernels: 110 us -> 105 us  [per_device(): pl.pallas_call(functools.partial(step_kernel, n, nrow), out_shape=(jax.Sh...]
where the time goes in v2:
time: 108 us
  Pallas kernels  105 us (97%)
  local copies, waits for them, and re-layouts  2.32 us (2%)
    pallas_call x1, Pallas kernels, per_device(): pl.pallas_call(functools.partial(step_kernel, n, nrow), out_shape=(jax.Sh...  105 us
    unnamed x4, local copies, waits for them, and re-layouts  2.32 us

profile of v2, /device:TPU:1, one launch (start us, length us, event | category | flops | bytes accessed | tf_op | source)
XLA Modules:
  0.0 107.5 jit_solution(17135237359621062666)
XLA Ops:
  0.6 104.5 %block_step.1 = (bf16[512,128]{1,0:T(8,128)(2,1)}, bf16[512,256]{1,0:T(8,128)(2,1)}) custom-call(bf16[512,128]{1,0:T(8,128)(2,1)} %res_hbm.1, f32[16,128]{1,0:T(8,128)} %bitcast.5, bf16[128,384]{1,0:T(8,128)(2,1)} %wg_hbm.1, bf16[128,384]{1,0:T(8,128)(2,1)} %wu_hbm.1, bf16[384,128]{1,0:T(8,128)(2,1)} %wd_hbm.1, f32[16,128]{1,0:T(8,128)} %bitcast.6, ...), custom_call_target="tpu_custom_call" | custom-call | tf_op jit(solution)/shard_map/block_step/pallas_call | solution.py:483
  105.2 0.0 copy-start
  105.2 1.6 %copy.14 = bf16[512,128]{1,0:T(8,128)(2,1)} copy(bf16[512,128]{1,0:T(8,128)(2,1)} %get-tuple-element.4) | data formatting | bytes 262144
  106.8 0.0 copy-done
  106.8 0.7 copy.15
Async XLA Ops:
  105.2 1.6 %copy-start = (bf16[512,256]{1,0:T(8,128)(2,1)S(1)}, bf16[512,256]{1,0:T(8,128)(2,1)}, u32[]{:S(2)}) copy-start(bf16[512,256]{1,0:T(8,128)(2,1)} %get-tuple-element.5) | copy-start | bytes 786436

commit v3 on v2

--- a/solution.py
+++ b/solution.py
@@ -24,7 +24,7 @@
     res_hbm, pg_hbm, wg_hbm, wu_hbm, wd_hbm, ng_hbm, wq_hbm, qg_hbm, kg_hbm, src_hbm,
     out_r, out_q,
     pg_ref, ng_ref, qg_ref, kg_ref, src_ref,
-    x, x2, wgu, wdn, wqk, gated, squares, proj, part, ring, first, onehot, rv, qv,
+    x, x2, wgu, wdn, wqk, hidden, gated, squares, proj, part, ring, first, onehot, rv, qv,
     a_send, a_recv, r_send, r_recv, b_send, b_recv,
     small, w_own, w1_send, w1_recv, w2_send, w2_recv, w3_send, w3_recv, p_send, p_recv,
 ):
@@ -43,7 +43,10 @@
     def ahead(k):
         return lax.rem(me + (k + 2 * n), n)
 
-    right, left = ahead(1), ahead(-1)
+    def along(d, k):
+        return ahead(k if d == 0 else -k)
+
+    onward = [along(0, 1), along(1, 1)]
 
     def rcopy(src, dst, ssem, rsem, **device):
         return pltpu.make_async_remote_copy(
@@ -68,7 +71,7 @@
         load.start()
 
     barrier = pltpu.get_barrier_semaphore()
-    greeted = [dict(col=right), dict(col=left), dict(rep=1 - rep)]
+    greeted = [dict(col=onward[0]), dict(col=onward[1]), dict(rep=1 - rep)]
     greeted += [dict(row=x_peer(j)) for j in range(1, NX)]
     greeted += [dict(row=y_peer(j)) for j in range(1, ny)]
     for device in greeted:
@@ -89,33 +92,24 @@
         return [(d, k) for d, k in chains if h * tm <= k * ch < (h + 1) * tm]
 
     def gather_hop(buf, send, recv, d, k, s):
-        blk = buf.at[ahead(-s if d == 0 else s), rows_of(k)]
-        return rcopy(blk, blk, send.at[d, s, k], recv.at[d, s, k], col=right if d == 0 else left)
+        blk = buf.at[along(d, -s), rows_of(k)]
+        return rcopy(blk, blk, send.at[d, s, k], recv.at[d, s, k], col=onward[d])
 
     def gather_arrival(buf, send, recv, d, k, s):
-        blk = buf.at[ahead(-1 - s if d == 0 else 1 + s), rows_of(k)]
-        return rcopy(blk, blk, send.at[d, s, k], recv.at[d, s, k], col=right if d == 0 else left)
-
-    def first_hop(d, k):
-        return rcopy(
-            res_hbm.at[rows_of(k)], x.at[me, rows_of(k)], a_send.at[d, 0, k], a_recv.at[d, 0, k],
-            col=right if d == 0 else left,
-        )
+        blk = buf.at[along(d, -1 - s), rows_of(k)]
+        return rcopy(blk, blk, send.at[d, s, k], recv.at[d, s, k], col=onward[d])
 
     def gather_step(buf, send, recv, s, group):
         for d, k in group:
             gather_arrival(buf, send, recv, d, k, s).wait_recv()
-            if not isinstance(s, int) or s + 1 < hops(d, k):
+            if s + 1 < hops(d, k):
                 gather_hop(buf, send, recv, d, k, s + 1).start()
 
     def gather_steps(buf, send, recv, lo, hi, extra=None):
-        def body(s, carry):
+        for s in range(lo, hi):
             gather_step(buf, send, recv, s, chains)
             if extra is not None:
                 extra(s)
-            return carry
-
-        lax.fori_loop(lo, hi, body, 0)
 
     def last_arrivals(buf, send, recv, group):
         for d, k in group:
@@ -124,7 +118,7 @@
 
     def sent(make, s):
         for d, k in chains:
-            if not isinstance(s, int) or s < hops(d, k):
+            if s < hops(d, k):
                 make(d, k, s).wait_send()
 
     half_ff, half_q = ff // 2, qkw // 2
@@ -270,11 +264,11 @@
         for c in range(2):
             gated[c, rows, :] = both[c]
 
-    stage_one((0,))
+    loads[0].wait()
     for d, k in chains:
-        first_hop(d, k).start()
-    stage_one((1,))
-    for load in loads:
+        gather_hop(x, a_send, a_recv, d, k, 0).start()
+    stage_one((0, 1))
+    for load in loads[1:]:
         load.wait()
     gather_step(x, a_send, a_recv, 0, chains)
     stage_two((0,))
@@ -308,23 +302,32 @@
         gate_up_add(h, (3, 4, 5, 6), False)
 
     def sum_first(d, k):
-        to = ahead(hops(d, k) if d == 0 else -hops(d, k))
+        to = along(d, hops(d, k))
         return to, rcopy(
             first.at[d, k], ring.at[d, 0, k], r_send.at[d, 0, k], r_recv.at[d, 0, k],
-            col=right if d == 0 else left,
+            col=onward[d],
         )
 
     def sum_hop(d, k, s):
         return rcopy(
             ring.at[d, s - 1, k], ring.at[d, s, k], r_send.at[d, s, k], r_recv.at[d, s, k],
-            col=right if d == 0 else left,
+            col=onward[d],
         )
 
     def sum_arrival(d, k, s):
         return rcopy(
             ring.at[d, s, k], ring.at[d, s, k], r_send.at[d, s, k], r_recv.at[d, s, k],
-            col=right if d == 0 else left,
+            col=onward[d],
         )
+
+    far_line = lax.rem(me + most - 1, n) // NX
+
+    def down_lines(h, lines):
+        for i in lines:
+            y = lax.rem(far_line + i, ny)
+            value = jnp.dot(hidden[pl.ds(h * tm, tm), :], wdn[y], preferred_element_type=F32)
+            for q in range(NX):
+                part[y * NX + q, pl.ds(h * tm, tm), :] = value[:, q * feat : (q + 1) * feat]
 
     for h in range(halves):
         last_arrivals(x, a_send, a_recv, in_half(h))
@@ -332,22 +335,21 @@
         scale = row_scale(square)
         gate = gate * scale
         up = up * scale
-        hidden = (gate / (1.0 + jnp.exp(-gate)) * up).astype(BF16)
+        hidden[pl.ds(h * tm, tm), :] = (gate / (1.0 + jnp.exp(-gate)) * up).astype(BF16)
         if h == 0:
             weights_here((1,))
-        for y in range(ny):
-            value = jnp.dot(hidden, wdn[y], preferred_element_type=F32)
-            for q in range(NX):
-                part[y * NX + q, pl.ds(h * tm, tm), :] = value[:, q * feat : (q + 1) * feat]
+        down_lines(h, (0, 1))
         for d, k in in_half(h):
             to, copy = sum_first(d, k)
             first[d, k] = part[to, rows_of(k), :].astype(BF16)
             copy.start()
+    for h in range(halves):
+        down_lines(h, range(2, ny))
     stage_one((2,))
 
     def sum_forward(d, k, s):
         sum_arrival(d, k, s - 1).wait_recv()
-        to = ahead(hops(d, k) - s if d == 0 else s - hops(d, k))
+        to = along(d, hops(d, k) - s)
         ring[d, s - 1, k] = (ring[d, s - 1, k].astype(F32) + part[to, rows_of(k), :]).astype(BF16)
         sum_hop(d, k, s).start()
 
@@ -355,19 +357,14 @@
         return gather_hop(x, a_send, a_recv, d, k, s)
 
     def sum_steps(lo, hi):
-        def body(s, carry):
+        for s in range(lo, hi):
             for d, k in chains:
                 sum_forward(d, k, s)
             sent(a_hop, s - 1)
-            return carry
-
-        lax.fori_loop(lo, hi, body, 0)
 
     sum_steps(1, 3)
     stage_two((2,))
     sum_steps(3, most - 1)
-    for k in range(tok // HD):
-        select_rows(k)
     for d, k in chains:
         if hops(d, k) == most:
             sum_forward(d, k, most - 1)
@@ -399,8 +396,7 @@
 
     stage_three((2,))
 
-    def qkv_part(rows, s, fresh):
-        blocks = pair(s)
+    def qkv_part(rows, blocks, fresh):
         square, lhs = taken(x2, ng_ref, blocks, rows)
         rhs = jnp.concatenate([wqk[b // NX, lax.rem(b, NX)] for b in blocks], axis=0)
         value = jnp.dot(lhs, rhs, preferred_element_type=F32)
@@ -412,9 +408,11 @@
     def qkv_add(s, fresh):
         for h in range(halves):
             rows = pl.ds(h * tm, tm)
-            square, value = qkv_part(rows, s, fresh)
+            square, value = qkv_part(rows, pair(s), fresh)
             squares[rows, :] = square
             proj[rows, :] = value
+
+    quarters = tok // HD
 
     def b_hop(d, k, s):
         return gather_hop(x2, b_send, b_recv, d, k, s)
@@ -430,7 +428,12 @@
         sent(sum_arrival, s)
         sent(b_hop, s - 1)
 
-    gather_steps(x2, b_send, b_recv, 1, most - 3, later)
+    def later_select(s):
+        later(s)
+        for k in range(quarters * (s - 1) // (most - 4), quarters * s // (most - 4)):
+            select_rows(k)
+
+    gather_steps(x2, b_send, b_recv, 1, most - 3, later_select)
     for k in range(CHUNKS):
         resid_copy(k).wait_recv()
     out_r[...] = (
@@ -444,21 +447,19 @@
     sent(sum_arrival, most - 1)
     sent(b_hop, most - 3)
 
-    for h in range(halves):
-        last_arrivals(x2, b_send, b_recv, in_half(h))
-        rows = pl.ds(h * tm, tm)
-        square, projected = qkv_part(rows, None, False)
+    for k in range(CHUNKS):
+        last_arrivals(x2, b_send, b_recv, [(d, i) for d, i in chains if i == k])
+        rows = rows_of(k)
+        square, projected = qkv_part(rows, pair(None), False)
         projected = projected * row_scale(square)
         for i in range(qkw // HD):
             head = me * (qkw // HD) + i
             value = projected[:, i * HD : (i + 1) * HD]
             scale = lax.rsqrt(jnp.mean(value * value, axis=-1, keepdims=True) + epsilon)
             gain = jnp.where(jnp.full((1, HD), head, jnp.int32) < HEADS, qg_ref[...], kg_ref[...])
-            normal = jnp.full((tm, HD), head, jnp.int32) < HEADS + KV_HEADS
+            normal = jnp.full((ch, HD), head, jnp.int32) < HEADS + KV_HEADS
             qv[0, rows, i * HD : (i + 1) * HD] = jnp.where(normal, value * scale * gain, value).astype(BF16)
-        for k in range(CHUNKS):
-            if h * tm <= k * ch < (h + 1) * tm:
-                qkv_copy(k).start()
+        qkv_copy(k).start()
 
     own_rows = jnp.dot(onehot[:, :tok], qv[0], preferred_element_type=F32)
     sent(b_hop, most - 2)
@@ -499,6 +500,7 @@
             pltpu.VMEM((2, ny, NX, feat, ff), BF16),
             pltpu.VMEM((ny, ff, NX * feat), BF16),
             pltpu.VMEM((ny, NX, feat, qkw), BF16),
+            pltpu.VMEM((tok, ff), BF16),
             pltpu.VMEM((2, tok, ff), F32),
             pltpu.VMEM((tok, feat), F32),
             pltpu.VMEM((tok, qkw), F32),

time: 108 us -> 107 us (level)
  no operation moved by 1% of the time
where the time goes in v3:
time: 107 us
  Pallas kernels  104 us (97%)
  local copies, waits for them, and re-layouts  2.32 us (2%)
    pallas_call x1, Pallas kernels, per_device(): pl.pallas_call(functools.partial(step_kernel, n, nrow), out_shape=(jax.Sh...  104 us
    unnamed x4, local copies, waits for them, and re-layouts  2.32 us

profile of v3, /device:TPU:1, one launch (start us, length us, event | category | flops | bytes accessed | tf_op | source)
XLA Modules:
  0.0 107.3 jit_solution(9870553058619919804)
XLA Ops:
  0.6 104.3 %block_step.1 = (bf16[512,128]{1,0:T(8,128)(2,1)}, bf16[512,256]{1,0:T(8,128)(2,1)}) custom-call(bf16[512,128]{1,0:T(8,128)(2,1)} %res_hbm.1, f32[16,128]{1,0:T(8,128)} %bitcast.5, bf16[128,384]{1,0:T(8,128)(2,1)} %wg_hbm.1, bf16[128,384]{1,0:T(8,128)(2,1)} %wu_hbm.1, bf16[384,128]{1,0:T(8,128)(2,1)} %wd_hbm.1, f32[16,128]{1,0:T(8,128)} %bitcast.6, ...), custom_call_target="tpu_custom_call" | custom-call | tf_op jit(solution)/shard_map/block_step/pallas_call | solution.py:484
  104.9 0.0 copy-start
  104.9 1.6 %copy.14 = bf16[512,128]{1,0:T(8,128)(2,1)} copy(bf16[512,128]{1,0:T(8,128)(2,1)} %get-tuple-element.4) | data formatting | bytes 262144
  106.5 0.0 copy-done
  106.6 0.7 copy.15
Async XLA Ops:
  104.9 1.6 %copy-start = (bf16[512,256]{1,0:T(8,128)(2,1)S(1)}, bf16[512,256]{1,0:T(8,128)(2,1)}, u32[]{:S(2)}) copy-start(bf16[512,256]{1,0:T(8,128)(2,1)} %get-tuple-element.5) | copy-start | bytes 786436

commit v4 on v3

--- a/solution.py
+++ b/solution.py
@@ -47,6 +47,7 @@
         return ahead(k if d == 0 else -k)
 
     onward = [along(0, 1), along(1, 1)]
+    beyond = [along(0, 2), along(1, 2)]
 
     def rcopy(src, dst, ssem, rsem, **device):
         return pltpu.make_async_remote_copy(
@@ -71,7 +72,7 @@
         load.start()
 
     barrier = pltpu.get_barrier_semaphore()
-    greeted = [dict(col=onward[0]), dict(col=onward[1]), dict(rep=1 - rep)]
+    greeted = [dict(col=c) for c in onward + beyond] + [dict(rep=1 - rep)]
     greeted += [dict(row=x_peer(j)) for j in range(1, NX)]
     greeted += [dict(row=y_peer(j)) for j in range(1, ny)]
     for device in greeted:
@@ -102,8 +103,11 @@
     def gather_step(buf, send, recv, s, group):
         for d, k in group:
             gather_arrival(buf, send, recv, d, k, s).wait_recv()
-            if s + 1 < hops(d, k):
+            if s + 1 < most - 1:
                 gather_hop(buf, send, recv, d, k, s + 1).start()
+            if s == most - 3 and hops(d, k) == most:
+                blk = buf.at[along(d, -1 - s), rows_of(k)]
+                rcopy(blk, blk, send.at[d, most - 1, k], recv.at[d, most - 1, k], col=beyond[d]).start()
 
     def gather_steps(buf, send, recv, lo, hi, extra=None):
         for s in range(lo, hi):

time: 107 us -> 107 us (level)
  no operation moved by 1% of the time
where the time goes in v4:
time: 107 us
  Pallas kernels  104 us (97%)
  local copies, waits for them, and re-layouts  2.32 us (2%)
    pallas_call x1, Pallas kernels, per_device(): pl.pallas_call(functools.partial(step_kernel, n, nrow), out_shape=(jax.Sh...  104 us
    unnamed x4, local copies, waits for them, and re-layouts  2.32 us

profile of v4, /device:TPU:1, one launch (start us, length us, event | category | flops | bytes accessed | tf_op | source)
XLA Modules:
  0.0 106.8 jit_solution(240964263431288252)
XLA Ops:
  0.6 103.8 %block_step.1 = (bf16[512,128]{1,0:T(8,128)(2,1)}, bf16[512,256]{1,0:T(8,128)(2,1)}) custom-call(bf16[512,128]{1,0:T(8,128)(2,1)} %res_hbm.1, f32[16,128]{1,0:T(8,128)} %bitcast.5, bf16[128,384]{1,0:T(8,128)(2,1)} %wg_hbm.1, bf16[128,384]{1,0:T(8,128)(2,1)} %wu_hbm.1, bf16[384,128]{1,0:T(8,128)(2,1)} %wd_hbm.1, f32[16,128]{1,0:T(8,128)} %bitcast.6, ...), custom_call_target="tpu_custom_call" | custom-call | tf_op jit(solution)/shard_map/block_step/pallas_call | solution.py:488
  104.5 0.0 copy-start
  104.5 1.6 %copy.14 = bf16[512,128]{1,0:T(8,128)(2,1)} copy(bf16[512,128]{1,0:T(8,128)(2,1)} %get-tuple-element.4) | data formatting | bytes 262144
  106.1 0.0 copy-done
  106.1 0.7 copy.15
Async XLA Ops:
  104.5 1.6 %copy-start = (bf16[512,256]{1,0:T(8,128)(2,1)S(1)}, bf16[512,256]{1,0:T(8,128)(2,1)}, u32[]{:S(2)}) copy-start(bf16[512,256]{1,0:T(8,128)(2,1)} %get-tuple-element.5) | copy-start | bytes 786436
